TPU v7x, 512 devices: a whole 4x8x8 slice. The times are simulated.
512 devices in a mesh: tok: 64 (over y_lo, z, core), head: 8 (over y_hi, x).
Axes of the slice: x: 4, y: 8 (y_hi: 2, y_lo: 4; y = y_hi * 4 + y_lo), z: 8, core: 2. Of those that a mesh axis runs over, the one named last changes fastest.
Arguments:
- queries: bfloat16 [65536, 4096], P(('tok', 'head')), may hold values from -60 to 60
- key_states: bfloat16 [65536, 1024], P(('tok', 'head')), may hold values from -60 to 60
- value_states: bfloat16 [65536, 1024], P(('tok', 'head')), may hold values from -6 to 6
- query_gain: float32 [128], replicated, may hold values from 0.5 to 6
- key_gain: float32 [128], replicated, may hold values from 0.5 to 6
- lengths: int32 [32], replicated, may hold values from 1 to 4096, as said below
- slot_order: int32 [64, 96], P('tok'), may hold values from 0 to 95, each once within a row
Outputs:
- attention: bfloat16 [65536, 4096], P('tok', 'head')
- page_pool: bfloat16 [6144, 16, 8, 256], P('tok', None, 'head')
Inputs may be any that keep to these rules, and one draw needn't show every extreme that they name: `lengths`: they sum to 65536; the first is 8 and the second exactly 4096. `slot_order`: each row is a permutation of the 96 slots.
All inputs are finite; a program needn't handle non-finite values.
Results may differ from a plain program's by a relative error of at most 0.0044.
The roundings to bfloat16 on the way count: a program that leaves them out, or rounds other values in their place, can miss the bound.
Values may be sent and summed in bfloat16 or wider, within the bound.
A program may use at most 64 MiB of HBM per device.

v0:
```python
import math

import jax
import jax.numpy as jnp
from jax import lax
from jax.sharding import PartitionSpec as P

HEAD_DIM = 128
REACH = 4
PAGE = 16


def from_behind(x, axis, by):
    peers = lax.axis_size(axis)
    pairs = [(i, i + by) for i in range(peers) if 0 <= i + by < peers]
    return lax.ppermute(x, axis, pairs)


def seg_table(lengths):
    seg_ends = jnp.cumsum(lengths)
    seg_starts = seg_ends - lengths
    return (seg_starts, seg_ends)


def locate(points, seg_starts, seg_ends):
    segment = jnp.sum((points[:, None] >= seg_starts[None, :]).astype(jnp.int32), axis=1) - 1
    onehot = segment[:, None] == jnp.arange(seg_starts.shape[0], dtype=jnp.int32)[None, :]
    first = jnp.sum(jnp.where(onehot, seg_starts[None, :], 0), axis=1)
    finish = jnp.sum(jnp.where(onehot, seg_ends[None, :], 0), axis=1)
    return (segment, first, finish)


def rms_scale(tensor, gain_vec):
    power_mean = jnp.mean(tensor * tensor, axis=-1, keepdims=True)
    return tensor * lax.rsqrt(power_mean + 1e-06) * gain_vec


def rotary(tensor, offset):
    half_dim = tensor.shape[-1] // 2
    frequency = jnp.exp(
        jnp.arange(half_dim, dtype=jnp.float32) * (-2.0 * math.log(1000000.0) / tensor.shape[-1])
    )
    angles = offset.astype(jnp.float32)[:, None] * frequency[None, :]
    cosine = jnp.concatenate([jnp.cos(angles), jnp.cos(angles)], axis=-1)[:, None, :]
    sine_rows = jnp.concatenate([jnp.sin(angles), jnp.sin(angles)], axis=-1)[:, None, :]
    turned = jnp.concatenate([-tensor[..., half_dim:], tensor[..., :half_dim]], axis=-1)
    return tensor * cosine + turned * sine_rows


def on_device(queries, key_states, value_states, query_gain, key_gain, lengths, slot_order):
    q_local, k_local, v_local = (
        lax.all_to_all(queries, "head", split_axis=1, concat_axis=0, tiled=True),
        lax.all_to_all(key_states, "head", split_axis=1, concat_axis=0, tiled=True),
        lax.all_to_all(value_states, "head", split_axis=1, concat_axis=0, tiled=True),
    )
    head_dim = HEAD_DIM
    shard_rows = q_local.shape[0]
    q_heads = q_local.shape[1] // head_dim
    kv_local = k_local.shape[1] // head_dim
    group_size = q_heads // kv_local
    tok_index = lax.axis_index("tok")
    base_row = tok_index * shard_rows
    seg_starts, seg_ends = seg_table(lengths)
    points = base_row + jnp.arange(shard_rows, dtype=jnp.int32)
    segment, first, finish = locate(points, seg_starts, seg_ends)
    offset = points - first
    q_rot = rotary(
        rms_scale(q_local.astype(jnp.float32).reshape(shard_rows, q_heads, head_dim), query_gain),
        offset,
    ).astype(jnp.bfloat16)
    k_rot = rotary(
        rms_scale(k_local.astype(jnp.float32).reshape(shard_rows, kv_local, head_dim), key_gain),
        offset,
    ).astype(jnp.bfloat16)
    paired = jnp.concatenate([k_rot, v_local.reshape(shard_rows, kv_local, head_dim)], axis=-1)
    sources = [(paired, 0)]
    for distance in range(1, REACH + 1):
        sources.append((from_behind(paired, "tok", distance), distance))
    block_rows = min(128, shard_rows)
    blocks = shard_rows // block_rows
    score_scale = 1.0 / math.sqrt(head_dim)
    key_info = []
    for source, distance in sources:
        key_points = base_row - distance * shard_rows + jnp.arange(shard_rows, dtype=jnp.int32)
        key_info.append((source, key_points, locate(key_points, seg_starts, seg_ends)[0]))

    def attend(inputs):
        query_tile, query_pos, query_seg = inputs
        state = (
            jnp.full((kv_local, block_rows, group_size), -1e30, jnp.float32),
            jnp.zeros((kv_local, block_rows, group_size), jnp.float32),
            jnp.zeros((kv_local, block_rows, group_size, head_dim), jnp.float32),
        )
        for source, key_points, key_seg in key_info:
            visible = (query_seg[:, None] == key_seg[None, :]) & (
                key_points[None, :] <= query_pos[:, None]
            )

            def update(current, source=source, visible=visible):
                run_max, run_sum, accum = current
                scores = (
                    jnp.einsum(
                        "qgrd,kgd->gqrk",
                        query_tile,
                        source[..., :head_dim],
                        preferred_element_type=jnp.float32,
                    )
                    * score_scale
                )
                masked = visible[None, :, None, :]
                scores = jnp.where(masked, scores, -1e30)
                new_max = jnp.maximum(run_max, jnp.max(scores, axis=-1))
                expo = jnp.where(masked, jnp.exp(scores - new_max[..., None]), 0.0)
                factor = jnp.exp(run_max - new_max)
                run_sum = run_sum * factor + jnp.sum(expo, axis=-1)
                mixed = jnp.einsum(
                    "gqrk,kgd->gqrd",
                    expo.astype(jnp.bfloat16),
                    source[..., head_dim:],
                    preferred_element_type=jnp.float32,
                )
                accum = accum * factor[..., None] + mixed
                return (new_max, run_sum, accum)

            state = lax.cond(jnp.any(visible), update, lambda current: current, state)
        run_max, run_sum, accum = state
        return accum / run_sum[..., None]

    tiles = q_rot.reshape(blocks, block_rows, kv_local, group_size, head_dim)
    result = lax.map(
        attend, (tiles, points.reshape(blocks, block_rows), segment.reshape(blocks, block_rows))
    )
    attention = (
        jnp.transpose(result, (0, 2, 1, 3, 4))
        .reshape(shard_rows, q_heads * head_dim)
        .astype(jnp.bfloat16)
    )
    tail_rows = from_behind(paired[shard_rows - PAGE :], "tok", 1)
    extended = jnp.concatenate([tail_rows, paired], axis=0)
    ext_points = base_row - PAGE + jnp.arange(PAGE + shard_rows, dtype=jnp.int32)
    ext_segment, ext_first, ext_finish = locate(ext_points, seg_starts, seg_ends)
    ext_offset = ext_points - ext_first
    page_last = jnp.minimum(ext_first + (ext_offset // PAGE + 1) * PAGE, ext_finish) - 1
    owned = (ext_segment >= 0) & (page_last // shard_rows == tok_index)
    page_ends = (offset % PAGE == PAGE - 1) | (points == finish - 1)
    flags = page_ends.astype(jnp.int32)
    before = jnp.cumsum(flags) - flags
    local_last = jnp.clip(page_last - base_row, 0, shard_rows - 1)
    rank_rows = before[local_last]
    pool_pages = slot_order.shape[1]
    slot_ids = jnp.sum(
        jnp.where(
            rank_rows[:, None] == jnp.arange(pool_pages, dtype=jnp.int32)[None, :],
            slot_order[0][None, :],
            0,
        ),
        axis=1,
    )
    target = jnp.where(owned, slot_ids * PAGE + ext_offset % PAGE, pool_pages * PAGE)
    page_pool = (
        jnp.zeros((pool_pages * PAGE, kv_local, 2 * head_dim), jnp.bfloat16)
        .at[target]
        .set(extended, mode="drop")
    )
    page_pool = page_pool.reshape(pool_pages, PAGE, kv_local, 2 * head_dim)
    return (attention, page_pool)


def solution(mesh):
    in_specs = (
        P(("tok", "head"), None),
        P(("tok", "head"), None),
        P(("tok", "head"), None),
        P(),
        P(),
        P(),
        P("tok", None),
    )
    out_specs = (P("tok", "head"), P("tok", None, "head", None))
    return jax.shard_map(
        on_device, mesh=mesh, in_specs=in_specs, out_specs=out_specs, check_vma=False
    )
```

profile of v0, /device:TPU:308, one launch (start us, length us, event | category | flops | bytes accessed | tf_op | source)
XLA Modules:
  0.0 296.3 jit_solution(2410883994028906601)
XLA Ops:
  2.3 9.6 %all-to-all-start.1 = ((bf16[128,8,128]{2,0,1:T(8,128)(2,1)}), bf16[128,8,128]{2,0,1:T(8,128)(2,1)S(1)}, u32[]{:S(2)}, u32[]{:S(2)}) async-start(bf16[128,8,128]{2,0,1:T(8,128)(2,1)} %copy_bitcast_fusion.2), calls=%async_computation.1 | async-start | bytes 524288 | tf_op jit(solution)/shard_map/all_to_all | solution.py:53
  16.9 4.4 %gather_fusion = s32[1040]{0:T(1024)S(1)} fusion(s32[1024]{0:T(1024)S(1)} %get-tuple-element.447, s32[2048]{0:T(1024)S(1)} %pad_clamp_fusion), kind=kCustom, calls=%fused_computation | custom fusion | bytes 12480 | tf_op jit(solution)/shard_map/gather | solution.py:149
  22.2 9.6 %all-to-all-start.2 = ((bf16[128,8,128]{2,0,1:T(8,128)(2,1)}), bf16[128,8,128]{2,0,1:T(8,128)(2,1)S(1)}, u32[]{:S(2)}, u32[]{:S(2)}) async-start(bf16[128,8,128]{2,0,1:T(8,128)(2,1)} %copy_bitcast_fusion.1), calls=%async_computation.2 | async-start | bytes 524288 | tf_op jit(solution)/shard_map/all_to_all | solution.py:54
  33.2 4.8 %all-to-all-done.2 = bf16[128,8,128]{2,0,1:T(8,128)(2,1)S(1)} async-done(((bf16[128,8,128]{2,0,1:T(8,128)(2,1)}), bf16[128,8,128]{2,0,1:T(8,128)(2,1)S(1)}, u32[]{:S(2)}, u32[]{:S(2)}) %all-to-all-start.2) | async-done | bytes 262176 | tf_op jit(solution)/shard_map/all_to_all | solution.py:54
  38.0 10.8 %all-to-all-start = ((bf16[128,8,512]{0,2,1:T(8,128)(2,1)}), bf16[128,8,512]{0,2,1:T(8,128)(2,1)S(1)}, u32[]{:S(2)}, u32[]{:S(2)}) async-start(bf16[128,8,512]{0,2,1:T(8,128)(2,1)} %bitcast.50), calls=%async_computation | async-start | bytes 2097152 | tf_op jit(solution)/shard_map/all_to_all | solution.py:52
  66.6 9.6 %scatter_custom_fusion = bf16[1536,256]{1,0:T(8,128)(2,1)} fusion(s32[1040]{0:T(1024)S(1)} %fusion.122, bf16[1024,1,128]{2,0,1:T(8,128)(2,1)S(1)} %bitcast.249, bf16[]{:T(256)} %constant.183, bf16[1024,1,128]{2,0,1:T(8,128)(2,1)S(1)} %fusion.116, bf16[16,1,256]{2,0,1:T(8,128)(2,1)S(1)} %collective-permute-done.4, bf16[]{:T(256)} %constant.166.clone.1), kind=kCustom, calls=%fused_computation.155 | custom fusion | flops 1597440 | bytes 1318916 | tf_op jit(solution)/shard_map/scatter | solution.py:163
  88.8 26.7 %collective-permute-done.3 = bf16[1024,1,256]{2,0,1:T(8,128)(2,1)} collective-permute-done((bf16[1024,1,256]{2,0,1:T(8,128)(2,1)}, bf16[1024,1,256]{2,0,1:T(8,128)(2,1)}, u32[]{:S(2)}, u32[]{:S(2)}) %collective-permute-start.3) | collective-permute-done | bytes 524320 | tf_op jit(solution)/shard_map/ppermute | solution.py:16
  115.5 178.8 %while.11 = (s32[]{:T(128)}, bf16[8,1,128,4,128]{4,2,3,1,0:T(8,128)(2,1)S(1)}, s32[8,128]{1,0:T(8,128)S(1)}, s32[1024]{0:T(1024)S(1)}, s32[8,128]{1,0:T(8,128)S(...) while((s32[]{:T(128)}, ...), condition=%wide.region_35.36_spmd.clone, body=%wide.region_9.35_spmd.clone.sunk | while | flops 1379546624 | bytes 40982148 | solution.py:130
  124.2 4.1 %conditional.17 = ((f32[1,128,4]{1,2,0:T(4,128)S(1)}, f32[1,128,4]{1,2,0:T(4,128)S(1)}, f32[1,128,4,128]{3,1,2,0:T(8,128)S(1)})) conditional(s32[]{:T(128)} %convert_element_type.212, (f32[1,128,4]{1,2,0:T(4,128)S(1)}, f32[1,128,4]{1,2,0:T(4,128)S(1)}, f32[1,128,4,128]{3,1,2,0:T(8,128)S(1)}) %get-tuple-element.738, ...), branch_computations={%region_23.23_spmd, %region_24.26_spmd} | conditional | flops 275383808 | bytes 7897120 | solution.py:125
  129.0 4.1 %conditional.18 = ((f32[1,128,4]{1,2,0:T(4,128)S(1)}, f32[1,128,4]{1,2,0:T(4,128)S(1)}, f32[1,128,4,128]{3,1,2,0:T(8,128)S(1)})) conditional(s32[]{:T(128)} %convert_element_type.211, (f32[1,128,4]{1,2,0:T(4,128)S(1)}, f32[1,128,4]{1,2,0:T(4,128)S(1)}, f32[1,128,4,128]{3,1,2,0:T(8,128)S(1)}) %get-tuple-element.739, ...), branch_computations={%region_27.27_spmd, %region_28.30_spmd} | conditional | flops 275383808 | bytes 7897120 | solution.py:125
  133.6 4.1 %conditional.19 = ((f32[1,128,4]{1,2,0:T(4,128)S(1)}, f32[1,128,4,128]{3,1,2,0:T(8,128)S(1)})) conditional(s32[]{:T(128)} %convert_element_type.210, (f32[1,128,4]{1,2,0:T(4,128)S(1)}, f32[1,128,4,128]{3,1,2,0:T(8,128)S(1)}) %tuple.131, (pred[128,1024]{1,0:T(8,128)(4,1)S(1)}, bf16[128,1,4,128]{3,0,2,1:T(8,128)(2,1)S(1)}, ...), branch_computations={%region_31.31_spmd, %region_32.34_spmd} | conditional | flops 275383808 | bytes 7893016 | solution.py:125
  146.5 4.1 %conditional.17 = ((f32[1,128,4]{1,2,0:T(4,128)S(1)}, f32[1,128,4]{1,2,0:T(4,128)S(1)}, f32[1,128,4,128]{3,1,2,0:T(8,128)S(1)})) conditional(s32[]{:T(128)} %convert_element_type.212, (f32[1,128,4]{1,2,0:T(4,128)S(1)}, f32[1,128,4]{1,2,0:T(4,128)S(1)}, f32[1,128,4,128]{3,1,2,0:T(8,128)S(1)}) %get-tuple-element.738, ...), branch_computations={%region_23.23_spmd, %region_24.26_spmd} | conditional | flops 275383808 | bytes 7897120 | solution.py:125
  151.3 4.1 %conditional.18 = ((f32[1,128,4]{1,2,0:T(4,128)S(1)}, f32[1,128,4]{1,2,0:T(4,128)S(1)}, f32[1,128,4,128]{3,1,2,0:T(8,128)S(1)})) conditional(s32[]{:T(128)} %convert_element_type.211, (f32[1,128,4]{1,2,0:T(4,128)S(1)}, f32[1,128,4]{1,2,0:T(4,128)S(1)}, f32[1,128,4,128]{3,1,2,0:T(8,128)S(1)}) %get-tuple-element.739, ...), branch_computations={%region_27.27_spmd, %region_28.30_spmd} | conditional | flops 275383808 | bytes 7897120 | solution.py:125
  156.0 4.1 %conditional.19 = ((f32[1,128,4]{1,2,0:T(4,128)S(1)}, f32[1,128,4,128]{3,1,2,0:T(8,128)S(1)})) conditional(s32[]{:T(128)} %convert_element_type.210, (f32[1,128,4]{1,2,0:T(4,128)S(1)}, f32[1,128,4,128]{3,1,2,0:T(8,128)S(1)}) %tuple.131, (pred[128,1024]{1,0:T(8,128)(4,1)S(1)}, bf16[128,1,4,128]{3,0,2,1:T(8,128)(2,1)S(1)}, ...), branch_computations={%region_31.31_spmd, %region_32.34_spmd} | conditional | flops 275383808 | bytes 7893016 | solution.py:125
  168.9 4.1 %conditional.17 = ((f32[1,128,4]{1,2,0:T(4,128)S(1)}, f32[1,128,4]{1,2,0:T(4,128)S(1)}, f32[1,128,4,128]{3,1,2,0:T(8,128)S(1)})) conditional(s32[]{:T(128)} %convert_element_type.212, (f32[1,128,4]{1,2,0:T(4,128)S(1)}, f32[1,128,4]{1,2,0:T(4,128)S(1)}, f32[1,128,4,128]{3,1,2,0:T(8,128)S(1)}) %get-tuple-element.738, ...), branch_computations={%region_23.23_spmd, %region_24.26_spmd} | conditional | flops 275383808 | bytes 7897120 | solution.py:125
  173.7 4.1 %conditional.18 = ((f32[1,128,4]{1,2,0:T(4,128)S(1)}, f32[1,128,4]{1,2,0:T(4,128)S(1)}, f32[1,128,4,128]{3,1,2,0:T(8,128)S(1)})) conditional(s32[]{:T(128)} %convert_element_type.211, (f32[1,128,4]{1,2,0:T(4,128)S(1)}, f32[1,128,4]{1,2,0:T(4,128)S(1)}, f32[1,128,4,128]{3,1,2,0:T(8,128)S(1)}) %get-tuple-element.739, ...), branch_computations={%region_27.27_spmd, %region_28.30_spmd} | conditional | flops 275383808 | bytes 7897120 | solution.py:125
  178.3 4.1 %conditional.19 = ((f32[1,128,4]{1,2,0:T(4,128)S(1)}, f32[1,128,4,128]{3,1,2,0:T(8,128)S(1)})) conditional(s32[]{:T(128)} %convert_element_type.210, (f32[1,128,4]{1,2,0:T(4,128)S(1)}, f32[1,128,4,128]{3,1,2,0:T(8,128)S(1)}) %tuple.131, (pred[128,1024]{1,0:T(8,128)(4,1)S(1)}, bf16[128,1,4,128]{3,0,2,1:T(8,128)(2,1)S(1)}, ...), branch_computations={%region_31.31_spmd, %region_32.34_spmd} | conditional | flops 275383808 | bytes 7893016 | solution.py:125
  191.3 4.1 %conditional.17 = ((f32[1,128,4]{1,2,0:T(4,128)S(1)}, f32[1,128,4]{1,2,0:T(4,128)S(1)}, f32[1,128,4,128]{3,1,2,0:T(8,128)S(1)})) conditional(s32[]{:T(128)} %convert_element_type.212, (f32[1,128,4]{1,2,0:T(4,128)S(1)}, f32[1,128,4]{1,2,0:T(4,128)S(1)}, f32[1,128,4,128]{3,1,2,0:T(8,128)S(1)}) %get-tuple-element.738, ...), branch_computations={%region_23.23_spmd, %region_24.26_spmd} | conditional | flops 275383808 | bytes 7897120 | solution.py:125
  196.0 4.1 %conditional.18 = ((f32[1,128,4]{1,2,0:T(4,128)S(1)}, f32[1,128,4]{1,2,0:T(4,128)S(1)}, f32[1,128,4,128]{3,1,2,0:T(8,128)S(1)})) conditional(s32[]{:T(128)} %convert_element_type.211, (f32[1,128,4]{1,2,0:T(4,128)S(1)}, f32[1,128,4]{1,2,0:T(4,128)S(1)}, f32[1,128,4,128]{3,1,2,0:T(8,128)S(1)}) %get-tuple-element.739, ...), branch_computations={%region_27.27_spmd, %region_28.30_spmd} | conditional | flops 275383808 | bytes 7897120 | solution.py:125
  200.7 4.1 %conditional.19 = ((f32[1,128,4]{1,2,0:T(4,128)S(1)}, f32[1,128,4,128]{3,1,2,0:T(8,128)S(1)})) conditional(s32[]{:T(128)} %convert_element_type.210, (f32[1,128,4]{1,2,0:T(4,128)S(1)}, f32[1,128,4,128]{3,1,2,0:T(8,128)S(1)}) %tuple.131, (pred[128,1024]{1,0:T(8,128)(4,1)S(1)}, bf16[128,1,4,128]{3,0,2,1:T(8,128)(2,1)S(1)}, ...), branch_computations={%region_31.31_spmd, %region_32.34_spmd} | conditional | flops 275383808 | bytes 7893016 | solution.py:125
  213.6 4.1 %conditional.17 = ((f32[1,128,4]{1,2,0:T(4,128)S(1)}, f32[1,128,4]{1,2,0:T(4,128)S(1)}, f32[1,128,4,128]{3,1,2,0:T(8,128)S(1)})) conditional(s32[]{:T(128)} %convert_element_type.212, (f32[1,128,4]{1,2,0:T(4,128)S(1)}, f32[1,128,4]{1,2,0:T(4,128)S(1)}, f32[1,128,4,128]{3,1,2,0:T(8,128)S(1)}) %get-tuple-element.738, ...), branch_computations={%region_23.23_spmd, %region_24.26_spmd} | conditional | flops 275383808 | bytes 7897120 | solution.py:125
  218.4 4.1 %conditional.18 = ((f32[1,128,4]{1,2,0:T(4,128)S(1)}, f32[1,128,4]{1,2,0:T(4,128)S(1)}, f32[1,128,4,128]{3,1,2,0:T(8,128)S(1)})) conditional(s32[]{:T(128)} %convert_element_type.211, (f32[1,128,4]{1,2,0:T(4,128)S(1)}, f32[1,128,4]{1,2,0:T(4,128)S(1)}, f32[1,128,4,128]{3,1,2,0:T(8,128)S(1)}) %get-tuple-element.739, ...), branch_computations={%region_27.27_spmd, %region_28.30_spmd} | conditional | flops 275383808 | bytes 7897120 | solution.py:125
  223.0 4.1 %conditional.19 = ((f32[1,128,4]{1,2,0:T(4,128)S(1)}, f32[1,128,4,128]{3,1,2,0:T(8,128)S(1)})) conditional(s32[]{:T(128)} %convert_element_type.210, (f32[1,128,4]{1,2,0:T(4,128)S(1)}, f32[1,128,4,128]{3,1,2,0:T(8,128)S(1)}) %tuple.131, (pred[128,1024]{1,0:T(8,128)(4,1)S(1)}, bf16[128,1,4,128]{3,0,2,1:T(8,128)(2,1)S(1)}, ...), branch_computations={%region_31.31_spmd, %region_32.34_spmd} | conditional | flops 275383808 | bytes 7893016 | solution.py:125
  236.0 4.1 %conditional.17 = ((f32[1,128,4]{1,2,0:T(4,128)S(1)}, f32[1,128,4]{1,2,0:T(4,128)S(1)}, f32[1,128,4,128]{3,1,2,0:T(8,128)S(1)})) conditional(s32[]{:T(128)} %convert_element_type.212, (f32[1,128,4]{1,2,0:T(4,128)S(1)}, f32[1,128,4]{1,2,0:T(4,128)S(1)}, f32[1,128,4,128]{3,1,2,0:T(8,128)S(1)}) %get-tuple-element.738, ...), branch_computations={%region_23.23_spmd, %region_24.26_spmd} | conditional | flops 275383808 | bytes 7897120 | solution.py:125
  240.7 4.1 %conditional.18 = ((f32[1,128,4]{1,2,0:T(4,128)S(1)}, f32[1,128,4]{1,2,0:T(4,128)S(1)}, f32[1,128,4,128]{3,1,2,0:T(8,128)S(1)})) conditional(s32[]{:T(128)} %convert_element_type.211, (f32[1,128,4]{1,2,0:T(4,128)S(1)}, f32[1,128,4]{1,2,0:T(4,128)S(1)}, f32[1,128,4,128]{3,1,2,0:T(8,128)S(1)}) %get-tuple-element.739, ...), branch_computations={%region_27.27_spmd, %region_28.30_spmd} | conditional | flops 275383808 | bytes 7897120 | solution.py:125
  245.4 4.1 %conditional.19 = ((f32[1,128,4]{1,2,0:T(4,128)S(1)}, f32[1,128,4,128]{3,1,2,0:T(8,128)S(1)})) conditional(s32[]{:T(128)} %convert_element_type.210, (f32[1,128,4]{1,2,0:T(4,128)S(1)}, f32[1,128,4,128]{3,1,2,0:T(8,128)S(1)}) %tuple.131, (pred[128,1024]{1,0:T(8,128)(4,1)S(1)}, bf16[128,1,4,128]{3,0,2,1:T(8,128)(2,1)S(1)}, ...), branch_computations={%region_31.31_spmd, %region_32.34_spmd} | conditional | flops 275383808 | bytes 7893016 | solution.py:125
  258.3 4.1 %conditional.17 = ((f32[1,128,4]{1,2,0:T(4,128)S(1)}, f32[1,128,4]{1,2,0:T(4,128)S(1)}, f32[1,128,4,128]{3,1,2,0:T(8,128)S(1)})) conditional(s32[]{:T(128)} %convert_element_type.212, (f32[1,128,4]{1,2,0:T(4,128)S(1)}, f32[1,128,4]{1,2,0:T(4,128)S(1)}, f32[1,128,4,128]{3,1,2,0:T(8,128)S(1)}) %get-tuple-element.738, ...), branch_computations={%region_23.23_spmd, %region_24.26_spmd} | conditional | flops 275383808 | bytes 7897120 | solution.py:125
  263.1 4.1 %conditional.18 = ((f32[1,128,4]{1,2,0:T(4,128)S(1)}, f32[1,128,4]{1,2,0:T(4,128)S(1)}, f32[1,128,4,128]{3,1,2,0:T(8,128)S(1)})) conditional(s32[]{:T(128)} %convert_element_type.211, (f32[1,128,4]{1,2,0:T(4,128)S(1)}, f32[1,128,4]{1,2,0:T(4,128)S(1)}, f32[1,128,4,128]{3,1,2,0:T(8,128)S(1)}) %get-tuple-element.739, ...), branch_computations={%region_27.27_spmd, %region_28.30_spmd} | conditional | flops 275383808 | bytes 7897120 | solution.py:125
  267.8 4.1 %conditional.19 = ((f32[1,128,4]{1,2,0:T(4,128)S(1)}, f32[1,128,4,128]{3,1,2,0:T(8,128)S(1)})) conditional(s32[]{:T(128)} %convert_element_type.210, (f32[1,128,4]{1,2,0:T(4,128)S(1)}, f32[1,128,4,128]{3,1,2,0:T(8,128)S(1)}) %tuple.131, (pred[128,1024]{1,0:T(8,128)(4,1)S(1)}, bf16[128,1,4,128]{3,0,2,1:T(8,128)(2,1)S(1)}, ...), branch_computations={%region_31.31_spmd, %region_32.34_spmd} | conditional | flops 275383808 | bytes 7893016 | solution.py:125
  280.7 4.1 %conditional.17 = ((f32[1,128,4]{1,2,0:T(4,128)S(1)}, f32[1,128,4]{1,2,0:T(4,128)S(1)}, f32[1,128,4,128]{3,1,2,0:T(8,128)S(1)})) conditional(s32[]{:T(128)} %convert_element_type.212, (f32[1,128,4]{1,2,0:T(4,128)S(1)}, f32[1,128,4]{1,2,0:T(4,128)S(1)}, f32[1,128,4,128]{3,1,2,0:T(8,128)S(1)}) %get-tuple-element.738, ...), branch_computations={%region_23.23_spmd, %region_24.26_spmd} | conditional | flops 275383808 | bytes 7897120 | solution.py:125
  285.5 4.1 %conditional.18 = ((f32[1,128,4]{1,2,0:T(4,128)S(1)}, f32[1,128,4]{1,2,0:T(4,128)S(1)}, f32[1,128,4,128]{3,1,2,0:T(8,128)S(1)})) conditional(s32[]{:T(128)} %convert_element_type.211, (f32[1,128,4]{1,2,0:T(4,128)S(1)}, f32[1,128,4]{1,2,0:T(4,128)S(1)}, f32[1,128,4,128]{3,1,2,0:T(8,128)S(1)}) %get-tuple-element.739, ...), branch_computations={%region_27.27_spmd, %region_28.30_spmd} | conditional | flops 275383808 | bytes 7897120 | solution.py:125
  290.1 4.1 %conditional.19 = ((f32[1,128,4]{1,2,0:T(4,128)S(1)}, f32[1,128,4,128]{3,1,2,0:T(8,128)S(1)})) conditional(s32[]{:T(128)} %convert_element_type.210, (f32[1,128,4]{1,2,0:T(4,128)S(1)}, f32[1,128,4,128]{3,1,2,0:T(8,128)S(1)}) %tuple.131, (pred[128,1024]{1,0:T(8,128)(4,1)S(1)}, bf16[128,1,4,128]{3,0,2,1:T(8,128)(2,1)S(1)}, ...), branch_computations={%region_31.31_spmd, %region_32.34_spmd} | conditional | flops 275383808 | bytes 7893016 | solution.py:125
  (397 shorter events, 227.9 us)
Async XLA Ops:
  0.6 1.0 copy-start
  2.3 19.9 %all-to-all-start.1 = ((bf16[128,8,128]{2,0,1:T(8,128)(2,1)}), bf16[128,8,128]{2,0,1:T(8,128)(2,1)S(1)}, u32[]{:S(2)}, u32[]{:S(2)}) async-start(bf16[128,8,128]{2,0,1:T(8,128)(2,1)} %copy_bitcast_fusion.2), calls=%async_computation.1 | async-start | bytes 524288 | tf_op jit(solution)/shard_map/all_to_all | solution.py:53
  16.9 4.4 %copy-start.9 = (s32[1,96]{1,0:T(1,128)S(1)}, s32[1,96]{1,0:T(1,128)}, u32[]{:S(2)}) copy-start(s32[1,96]{1,0:T(1,128)} %param.25) | copy-start | bytes 1156
  16.9 4.5 %copy-start.6 = (bf16[128,1024]{1,0:T(8,128)(2,1)S(1)}, bf16[128,1024]{1,0:T(8,128)(2,1)}, u32[]{:S(2)}) copy-start(bf16[128,1024]{1,0:T(8,128)(2,1)} %param.21) | copy-start | bytes 786436
  16.9 14.9 %copy-start.4 = (bf16[128,4096]{1,0:T(8,128)(2,1)S(1)}, bf16[128,4096]{1,0:T(8,128)(2,1)}, u32[]{:S(2)}) copy-start(bf16[128,4096]{1,0:T(8,128)(2,1)} %param.19) | copy-start | bytes 3145732
  22.2 15.7 %all-to-all-start.2 = ((bf16[128,8,128]{2,0,1:T(8,128)(2,1)}), bf16[128,8,128]{2,0,1:T(8,128)(2,1)S(1)}, u32[]{:S(2)}, u32[]{:S(2)}) async-start(bf16[128,8,128]{2,0,1:T(8,128)(2,1)} %copy_bitcast_fusion.1), calls=%async_computation.2 | async-start | bytes 524288 | tf_op jit(solution)/shard_map/all_to_all | solution.py:54
  38.0 13.1 %copy-start.7 = (f32[128]{0:T(128)S(1)}, f32[128]{0:T(128)}, u32[]{:S(2)}) copy-start(f32[128]{0:T(128)} %param.23) | copy-start | bytes 1540
  38.0 38.2 %all-to-all-start = ((bf16[128,8,512]{0,2,1:T(8,128)(2,1)}), bf16[128,8,512]{0,2,1:T(8,128)(2,1)S(1)}, u32[]{:S(2)}, u32[]{:S(2)}) async-start(bf16[128,8,512]{0,2,1:T(8,128)(2,1)} %bitcast.50), calls=%async_computation | async-start | bytes 2097152 | tf_op jit(solution)/shard_map/all_to_all | solution.py:52
  52.1 14.4 %collective-permute-start.4 = (bf16[16,1,256]{2,0,1:T(8,128)(2,1)S(1)}, bf16[16,1,256]{2,0,1:T(8,128)(2,1)S(1)}, u32[]{:S(2)}, u32[]{:S(2)}) collective-permute-start(bf16[16,1,256]{2,0,1:T(8,128)(2,1)S(1)} %fusion.119), channel_id=1, source_target_pairs={{0,8},{8,16},{16,24},{24,32},{32,40},{40,48},{48,56},{56,64},{64,7... | collective-permute-start | bytes 24584 | tf_op jit(solution)/shard_map/ppermute | solution.py:16
  54.9 32.4 %collective-permute-start = (bf16[1024,1,256]{2,0,1:T(8,128)(2,1)}, bf16[1024,1,256]{2,0,1:T(8,128)(2,1)S(1)}, u32[]{:S(2)}, u32[]{:S(2)}) collective-permute-start(bf16[1024,1,256]{2,0,1:T(8,128)(2,1)} %pad_maximum_fusion), channel_id=1, source_target_pairs={{0,8},{8,16},{16,24},{24,32},{32,40},{40,48},{48,56},{56,64},{64,7... | collective-permute-start | bytes 1572872 | tf_op jit(solution)/shard_map/ppermute | solution.py:16
  58.4 28.9 %collective-permute-start.1 = (bf16[1024,1,256]{2,0,1:T(8,128)(2,1)}, bf16[1024,1,256]{2,0,1:T(8,128)(2,1)}, u32[]{:S(2)}, u32[]{:S(2)}) collective-permute-start(bf16[1024,1,256]{2,0,1:T(8,128)(2,1)} %pad_maximum_fusion), channel_id=1, source_target_pairs={{0,16},{8,24},{16,32},{24,40},{32,48},{40,56},{48,64},{56,72},{64,... | collective-permute-start | bytes 1572872 | tf_op jit(solution)/shard_map/ppermute | solution.py:16
  61.8 27.0 %collective-permute-start.2 = (bf16[1024,1,256]{2,0,1:T(8,128)(2,1)}, bf16[1024,1,256]{2,0,1:T(8,128)(2,1)}, u32[]{:S(2)}, u32[]{:S(2)}) collective-permute-start(bf16[1024,1,256]{2,0,1:T(8,128)(2,1)} %pad_maximum_fusion), channel_id=1, source_target_pairs={{0,24},{8,32},{16,40},{24,48},{32,56},{40,64},{48,72},{56,80},{64,... | collective-permute-start | bytes 1572872 | tf_op jit(solution)/shard_map/ppermute | solution.py:16
  64.5 51.0 %collective-permute-start.3 = (bf16[1024,1,256]{2,0,1:T(8,128)(2,1)}, bf16[1024,1,256]{2,0,1:T(8,128)(2,1)}, u32[]{:S(2)}, u32[]{:S(2)}) collective-permute-start(bf16[1024,1,256]{2,0,1:T(8,128)(2,1)} %pad_maximum_fusion), channel_id=1, source_target_pairs={{0,32},{8,40},{16,48},{24,56},{32,64},{40,72},{48,80},{56,88},{64,... | collective-permute-start | bytes 1572872 | tf_op jit(solution)/shard_map/ppermute | solution.py:16
  82.0 0.7 copy-start.8
  83.8 1.6 copy-start.1
  83.8 1.7 copy-start.2
  83.8 1.8 copy-start.3
  85.6 29.9 %copy-start.5 = (bf16[8,1,128,4,128]{4,2,3,1,0:T(8,128)(2,1)S(1)}, bf16[8,1,128,4,128]{4,2,3,1,0:T(8,128)(2,1)}, u32[]{:S(2)}) copy-start(bf16[8,1,128,4,128]{4,2,3,1,0:T(8,128)(2,1)} %custom-call.2) | copy-start | bytes 3145732
where the time goes:
time: 299 us; the launch traced here: 296 us
  matrix products  101 us (34%)
  other arithmetic  64.4 us (22%)
  starting transfers between devices  43.5 us (15%)
  waiting for transfers between devices  33 us (11%)
  loops' own time  26.6 us (9%)
  local copies, waits for them, and re-layouts  26.4 us (9%)
    dot_general x40, matrix products, update(): jnp.einsum('gqrk,kgd->gqrd', expo.astype(jnp.bfloat16), source[..., head_...  54.8 us
    dot_general x40, matrix products, update(): jnp.einsum('qgrd,kgd->gqrk', query_tile, source[..., :head_dim], preferre...  46.7 us
    reduce_sum x40, other arithmetic, update(): run_sum = run_sum * factor + jnp.sum(expo, axis=-1)  28.9 us
    ppermute x5, waiting for transfers between devices, from_behind(): return lax.ppermute(x, axis, pairs)  28.2 us
    another operation x1, loops' own time, on_device(): lax.map(attend, (tiles, points.reshape(blocks, block_rows), segment.resha...  25.6 us
    ppermute x5, starting transfers between devices, from_behind(): return lax.ppermute(x, axis, pairs)  13.5 us
    reduce_or x8, other arithmetic, attend(): state = lax.cond(jnp.any(visible), update, lambda current: current, state)  11 us
    all_to_all x1, starting transfers between devices, on_device(): lax.all_to_all(queries, 'head', split_axis=1, concat_axis=0, tiled=True)  10.8 us
  transfers between devices with their start and end apart: 8, of which 3 were waited for; matrix products, arithmetic and copies ran while one was open for 12% of the time, Pallas kernels for 0%

commit v1 on v0

v1 whole, which is shorter than its diff:
```python
import functools
import math

import jax
import jax.numpy as jnp
import numpy as np
from jax import lax
from jax.experimental import pallas as pl
from jax.experimental.pallas import tpu as pltpu
from jax.sharding import PartitionSpec as P

D = 128
REACH = 4
PAGE = 16
GROUP = 4
PEERS = 8
FAR = -1e30
MESH = pl.DeviceIdType.MESH
NT = (((1,), (1,)), ((), ()))


def kernel(
    n_tok,
    q_hbm,
    k_hbm,
    v_hbm,
    qg_ref,
    kg_ref,
    freq_ref,
    len_ref,
    slot_ref,
    out_hbm,
    pool_hbm,
    qin,
    kin,
    vin,
    kvs,
    qs,
    kv,
    qbuf,
    augk,
    augq,
    acc,
    peak,
    ostage,
    pstage,
    in_sem,
    own_sem,
    out_sem,
    kv_send,
    kv_recv,
    q_send,
    q_recv,
    z_send,
    z_recv,
    s_send,
    s_recv,
):
    rows = kin.shape[0]
    shard = rows * PEERS
    half = shard // 2
    segs = len_ref.shape[0]
    tok = lax.axis_index("tok")
    head = lax.axis_index("head")
    hi, x = head // 4, lax.rem(head, 4)
    core = lax.rem(tok, 2)
    sibling = tok + 1 - 2 * core
    base = tok * shard

    def dest(n):
        return (hi if n < 4 else 1 - hi) * 4 + lax.rem(x - n + 8, 4)

    def origin(n):
        return lax.rem(hi + n // 4, 2) * 4 + lax.rem(x + n, 4)

    def rows_of(chunk):
        return pl.ds(pl.multiple_of(chunk * rows, rows), rows)

    barrier = pltpu.get_barrier_semaphore()
    for n in range(1, PEERS):
        pl.semaphore_signal(barrier, device_id=(tok, dest(n)), device_id_type=MESH)
    pl.semaphore_signal(barrier, device_id=(sibling, head), device_id_type=MESH)

    @pl.when(tok + 2 < n_tok)
    def _():
        pl.semaphore_signal(barrier, device_id=(tok + 2, head), device_id_type=MESH)

    @pl.when(tok >= 2)
    def _():
        pl.semaphore_signal(barrier, device_id=(tok - 2, head), device_id_type=MESH)

    loads = [
        pltpu.make_async_copy(k_hbm, kin, in_sem.at[0]),
        pltpu.make_async_copy(v_hbm, vin, in_sem.at[1]),
        pltpu.make_async_copy(q_hbm, qin, in_sem.at[2]),
    ]
    for load in loads:
        load.start()

    lane = lax.broadcasted_iota(jnp.int32, (1, D), 1)
    starts = jnp.full((1, D), 1 << 30, jnp.int32)
    ends = starts
    total = jnp.int32(0)
    for s in range(segs):
        starts = jnp.where(lane == s, total, starts)
        total = total + len_ref[s]
        ends = jnp.where(lane == s, total, ends)

    place = base + head * rows + lax.broadcasted_iota(jnp.int32, (rows, 1), 0)
    inside = (place >= starts) & (place < ends)
    first = jnp.sum(jnp.where(inside, starts.astype(jnp.float32), 0.0), axis=1, keepdims=True)
    angle = (place.astype(jnp.float32) - first) * freq_ref[...]
    cosine = jnp.cos(angle)
    sine = jnp.sin(angle)
    sine = jnp.where(lax.broadcasted_iota(jnp.int32, (rows, D), 1) < D // 2, -sine, sine)

    def rotated(tensor, gain):
        tensor = tensor.astype(jnp.float32)
        power = jnp.mean(tensor * tensor, axis=1, keepdims=True)
        tensor = tensor * lax.rsqrt(power + 1e-6) * gain
        return (tensor * cosine + pltpu.roll(tensor, D // 2, 1) * sine).astype(jnp.bfloat16)

    loads[0].wait()
    for g in range(PEERS):
        kvs[g, 0] = rotated(kin[:, g * D : (g + 1) * D], kg_ref[...])
    loads[1].wait()
    for g in range(PEERS):
        kvs[g, 1] = vin[:, g * D : (g + 1) * D]

    pl.semaphore_wait(
        barrier,
        PEERS + (tok >= 2).astype(jnp.int32) + (tok + 2 < n_tok).astype(jnp.int32),
    )

    own_rows = pl.ds(pl.multiple_of(REACH * shard + head * rows, rows), rows)
    kv_copies = [pltpu.make_async_copy(kvs.at[head], kv.at[:, own_rows], own_sem.at[0])]
    q_copies = [pltpu.make_async_copy(qs.at[head], qbuf.at[0], own_sem.at[1])]
    for n in range(1, PEERS):
        kv_copies.append(
            pltpu.make_async_remote_copy(
                src_ref=kvs.at[dest(n)],
                dst_ref=kv.at[:, own_rows],
                send_sem=kv_send.at[n],
                recv_sem=kv_recv.at[n],
                device_id=(tok, dest(n)),
                device_id_type=MESH,
            )
        )
        q_copies.append(
            pltpu.make_async_remote_copy(
                src_ref=qs.at[dest(n)],
                dst_ref=qbuf.at[n],
                send_sem=q_send.at[n],
                recv_sem=q_recv.at[n],
                device_id=(tok, dest(n)),
                device_id_type=MESH,
            )
        )
    for n in (4, 5, 6, 7, 1, 2, 3, 0):
        kv_copies[n].start()

    loads[2].wait()

    def turn_queries(g, carry):
        for r in range(GROUP):
            cols = pl.ds(pl.multiple_of((g * GROUP + r) * D, D), D)
            qs[g, r * rows : (r + 1) * rows] = rotated(qin[:, cols], qg_ref[...])
        return carry

    lax.fori_loop(0, PEERS, turn_queries, 0)

    def slot_rows(d, part):
        return pl.ds(pl.multiple_of((REACH - d) * shard + part * half, half), half)

    parts = (hi, 1 - hi)

    def along(src_slot, dst_slot, which, index):
        return pltpu.make_async_remote_copy(
            src_ref=kv.at[:, slot_rows(src_slot, parts[which])],
            dst_ref=kv.at[:, slot_rows(dst_slot, parts[which])],
            send_sem=z_send.at[index],
            recv_sem=z_recv.at[index],
            device_id=(tok + 2, head),
            device_id_type=MESH,
        )

    def across(src_slot, dst_slot, which, index):
        return pltpu.make_async_remote_copy(
            src_ref=kv.at[:, slot_rows(src_slot, parts[which])],
            dst_ref=kv.at[:, slot_rows(dst_slot, parts[which])],
            send_sem=s_send.at[index],
            recv_sem=s_recv.at[index],
            device_id=(sibling, head),
            device_id_type=MESH,
        )

    def give(own, which):
        @pl.when(tok + 2 < n_tok)
        def _():
            if own:
                along(0, 2, which, which).start()
            else:

                @pl.when(tok >= 2)
                def _():
                    along(2, 4, which, 2 + which).start()

        if own:

            @pl.when(core == 0)
            def _():
                across(0, 1, which, which).start()
        else:

            @pl.when((core == 0) & (tok >= 2))
            def _():
                across(2, 3, which, 2 + which).start()

            @pl.when((core == 1) & (tok >= 2))
            def _():
                across(2, 1, which, which).start()

    for d in range(1, REACH + 1):

        @pl.when(tok < d)
        def _(d=d):
            kv[:, (REACH - d) * shard : (REACH - d + 1) * shard] = jnp.zeros((2, shard, D), jnp.bfloat16)

    for n in (1, 2, 3):
        q_copies[n].start()
    q_copies[0].start()
    for n in (1, 2, 3):
        kv_copies[n].wait_recv()
    kv_copies[0].wait()
    give(True, 0)
    for n in (4, 5, 6, 7):
        kv_copies[n].wait_recv()
    give(True, 1)
    for n in (4, 5, 6, 7):
        q_copies[n].start()

    def mark_keys(index, carry):
        point = base - REACH * shard + index * rows + lax.broadcasted_iota(jnp.int32, (rows, 1), 0)
        within = (point >= starts) & (point < ends)
        augk[rows_of(index)] = jnp.where(within, 0.0, FAR).astype(jnp.bfloat16)
        return carry

    lax.fori_loop(0, (REACH + 1) * PEERS, mark_keys, 0)

    def mark_queries(index, carry):
        point = base + index * rows + lax.broadcasted_iota(jnp.int32, (rows, 1), 0)
        within = (point >= starts) & (point < ends)
        augq[rows_of(index)] = jnp.where(within, 1.0, 0.0).astype(jnp.bfloat16)
        return carry

    lax.fori_loop(0, PEERS, mark_queries, 0)

    scale = math.log2(math.e) / math.sqrt(D)

    def tile(n, begin, length, opening):
        chunk = origin(n)
        mark = augq[rows_of(chunk)]
        query = jnp.concatenate([qbuf[n], jnp.concatenate([mark] * GROUP, axis=0)], axis=1)
        at = pl.ds(pl.multiple_of(chunk * rows + begin, rows), length)
        key = jnp.concatenate([kv[0, at], augk[at]], axis=1)
        value = jnp.concatenate([kv[1, at], jnp.ones((length, D), jnp.bfloat16)], axis=1)
        score = lax.dot_general(query, key, NT, preferred_element_type=jnp.float32)
        if opening:
            query_row = lax.rem(lax.broadcasted_iota(jnp.int32, score.shape, 0), rows)
            key_row = lax.broadcasted_iota(jnp.int32, score.shape, 1)
            score = jnp.where(key_row <= query_row, score, FAR)
        top = jnp.broadcast_to(jnp.max(score, axis=1, keepdims=True), (GROUP * rows, D))
        if not opening:
            old = peak[n]
            top = jnp.maximum(old, top)
        if length >= D:
            wide = jnp.concatenate([top] * (length // D), axis=1)
        else:
            wide = top[:, :length]
        expo = jnp.exp2((score - wide) * scale).astype(jnp.bfloat16)
        mixed = jnp.dot(expo, value, preferred_element_type=jnp.float32)
        if opening:
            acc[n] = mixed
        else:
            factor = jnp.exp2((old - top) * scale)
            acc[n] = acc[n] * jnp.concatenate([factor, factor], axis=1) + mixed
        peak[n] = top

    def tiles(low, high, begin, length, opening=False):
        def step(n, carry):
            tile(n, begin, length, opening)
            return carry

        lax.fori_loop(low, high, step, 0)

    def finish(n):
        done = acc[n]
        done = (done[:, :D] / done[:, D:]).astype(jnp.bfloat16)
        for r in range(GROUP):
            ostage[n, :, r * D : (r + 1) * D] = done[r * rows : (r + 1) * rows]

    def out_copy(n):
        return pltpu.make_async_copy(ostage.at[n], out_hbm.at[rows_of(origin(n))], out_sem.at[n])

    q_copies[0].wait()
    for n in (1, 2, 3):
        q_copies[n].wait_recv()
    tiles(0, 4, REACH * shard, rows, True)

    for which in (0, 1):

        @pl.when(tok >= 2)
        def _(which=which):
            along(0, 2, which, which).wait_recv()

        give(False, which)

    for which in (0, 1):

        @pl.when(tok >= 1)
        def _(which=which):
            across(0, 1, which, which).wait_recv()

    width = shard + 128
    spot = lax.broadcasted_iota(jnp.int32, (1, width), 1)
    point = base + spot - jnp.where(spot < shard, 0, width)
    begun = jnp.zeros((1, width), jnp.int32)
    ended = begun
    paged = begun
    total = jnp.int32(0)
    pages = jnp.int32(0)
    origin_rank = jnp.int32(0)
    for s in range(segs):
        length = len_ref[s]
        after = point >= total
        begun = jnp.where(after, total, begun)
        ended = jnp.where(after, total + length, ended)
        paged = jnp.where(after, pages, paged)
        origin_rank = jnp.where(base >= total, pages + lax.shift_right_logical(jnp.maximum(base - total, 0), 4), origin_rank)
        total = total + length
        pages = pages + lax.shift_right_logical(length + (PAGE - 1), 4)
    offset = jnp.maximum(point - begun, 0)
    block = lax.shift_right_logical(offset, 4)
    last = jnp.minimum(begun + (block + 1) * PAGE, ended) - 1
    owned = (point >= 0) & (last >= base) & (last < base + shard)
    wanted = jnp.where(owned, (paged + block - origin_rank) * PAGE + (offset & (PAGE - 1)), -1)

    pool_rows = pstage.shape[0]
    piece = 256
    slots = slot_ref[...]
    ranks = lax.broadcasted_iota(jnp.int32, slots.shape, 1).astype(jnp.float32)

    def fill(index, carry):
        row = index * piece + lax.broadcasted_iota(jnp.int32, (piece, 1), 0)
        rank = jnp.sum(jnp.where(slots == lax.shift_right_logical(row, 4), ranks, 0.0), axis=1, keepdims=True)
        code = rank.astype(jnp.int32) * PAGE + (row & (PAGE - 1))
        pick = jnp.where(code == wanted, 1.0, 0.0).astype(jnp.bfloat16)
        own = pl.ds(REACH * shard, shard)
        tail = pl.ds(REACH * shard - 128, 128)
        to = pl.ds(pl.multiple_of(index * piece, piece), piece)
        for plane in (0, 1):
            rowset = jnp.concatenate([kv[plane, own], kv[plane, tail]], axis=0)
            got = jnp.dot(pick, rowset, preferred_element_type=jnp.float32)
            pstage[to, plane * D : (plane + 1) * D] = got.astype(jnp.bfloat16)
        return carry

    lax.fori_loop(0, pool_rows // piece, fill, 0)
    pool_copy = pltpu.make_async_copy(pstage, pool_hbm, own_sem.at[2])
    pool_copy.start()

    tiles(0, 4, 3 * shard, shard)
    tiles(0, 4, 2 * shard, shard)

    for which in (0, 1):

        @pl.when(tok >= 4)
        def _(which=which):
            along(2, 4, which, 2 + which).wait_recv()

        @pl.when((core == 1) & (tok >= 4))
        def _(which=which):
            across(4, 3, which, 2 + which).start()

    for which in (0, 1):

        @pl.when(tok >= 3)
        def _(which=which):
            across(2, 3, which, 2 + which).wait_recv()

    def rest(n, carry):
        tile(n, 1 * shard, shard, False)
        tile(n, 0, shard, False)
        finish(n)
        out_copy(n).start()
        return carry

    lax.fori_loop(0, 4, rest, 0)

    for n in (4, 5, 6, 7):
        q_copies[n].wait_recv()

    def whole(n, carry):
        tile(n, REACH * shard, rows, True)
        lax.fori_loop(0, 4, lambda j, c: (tile(n, (3 - j) * shard, shard, False), c)[1], 0)
        finish(n)
        out_copy(n).start()
        return carry

    lax.fori_loop(4, 8, whole, 0)

    for n in range(1, PEERS):
        kv_copies[n].wait_send()
        q_copies[n].wait_send()
    for which in (0, 1):

        @pl.when(tok + 2 < n_tok)
        def _(which=which):
            along(0, 2, which, which).wait_send()

            @pl.when(tok >= 2)
            def _():
                along(2, 4, which, 2 + which).wait_send()

        @pl.when((core == 0) | (tok >= 2))
        def _(which=which):
            across(0, 1, which, which).wait_send()

        @pl.when(((core == 0) & (tok >= 2)) | ((core == 1) & (tok >= 4)))
        def _(which=which):
            across(2, 3, which, 2 + which).wait_send()

    for n in range(PEERS):
        out_copy(n).wait()
    pool_copy.wait()


def on_device(queries, key_states, value_states, query_gain, key_gain, lengths, slot_order):
    rows = queries.shape[0]
    shard = rows * PEERS
    slots = slot_order.shape[1]
    frequency = np.exp(np.arange(D // 2) * (-2.0 * math.log(1000000.0) / D)).astype(np.float32)
    frequency = jnp.asarray(np.concatenate([frequency, frequency])[None, :])
    vmem = pl.BlockSpec(memory_space=pltpu.VMEM)
    smem = pl.BlockSpec(memory_space=pltpu.SMEM)
    anywhere = pl.BlockSpec(memory_space=pl.ANY)
    bf16 = jnp.bfloat16
    dma = pltpu.SemaphoreType.DMA
    attention, pool = pl.pallas_call(
        functools.partial(kernel, lax.axis_size("tok")),
        out_shape=(
            jax.ShapeDtypeStruct((shard, GROUP * D), bf16),
            jax.ShapeDtypeStruct((slots * PAGE, 2 * D), bf16),
        ),
        in_specs=[anywhere, anywhere, anywhere, vmem, vmem, vmem, smem, vmem],
        out_specs=(anywhere, anywhere),
        scratch_shapes=[
            pltpu.VMEM((rows, PEERS * GROUP * D), bf16),
            pltpu.VMEM((rows, PEERS * D), bf16),
            pltpu.VMEM((rows, PEERS * D), bf16),
            pltpu.VMEM((PEERS, 2, rows, D), bf16),
            pltpu.VMEM((PEERS, GROUP * rows, D), bf16),
            pltpu.VMEM((2, (REACH + 1) * shard, D), bf16),
            pltpu.VMEM((PEERS, GROUP * rows, D), bf16),
            pltpu.VMEM(((REACH + 1) * shard, D), bf16),
            pltpu.VMEM((shard, D), bf16),
            pltpu.VMEM((PEERS, GROUP * rows, 2 * D), jnp.float32),
            pltpu.VMEM((PEERS, GROUP * rows, D), jnp.float32),
            pltpu.VMEM((PEERS, rows, GROUP * D), bf16),
            pltpu.VMEM((slots * PAGE, 2 * D), bf16),
            dma((3,)),
            dma((3,)),
            dma((PEERS,)),
            dma((PEERS,)),
            dma((PEERS,)),
            dma((PEERS,)),
            dma((PEERS,)),
            dma((4,)),
            dma((4,)),
            dma((4,)),
            dma((4,)),
        ],
        compiler_params=pltpu.CompilerParams(
            collective_id=0, has_side_effects=True, vmem_limit_bytes=56 * 2**20
        ),
        name="paged_prefill",
    )(
        queries,
        key_states,
        value_states,
        query_gain[None, :],
        key_gain[None, :],
        frequency,
        lengths,
        slot_order,
    )
    return attention, pool.reshape(slots, PAGE, 1, 2 * D)


def solution(mesh):
    in_specs = (
        P(("tok", "head"), None),
        P(("tok", "head"), None),
        P(("tok", "head"), None),
        P(),
        P(),
        P(),
        P("tok", None),
    )
    out_specs = (P("tok", "head"), P("tok", None, "head", None))
    return jax.shard_map(
        on_device, mesh=mesh, in_specs=in_specs, out_specs=out_specs, check_vma=False
    )
```

time: 299 us -> 115 us (0.38)
  the two profiles are of different devices: /device:TPU:308 before, /device:TPU:52 now
where the time goes in v1:
time: 115 us
  Pallas kernels  111 us (97%)
  local copies, waits for them, and re-layouts  3.22 us (3%)
    pallas_call x1, Pallas kernels, on_device(): pl.pallas_call(functools.partial(kernel, lax.axis_size('tok')), out_shape...  111 us
    unnamed x4, local copies, waits for them, and re-layouts  3.22 us

profile of v1, /device:TPU:52, one launch (start us, length us, event | category | flops | bytes accessed | tf_op | source)
XLA Modules:
  0.0 114.5 jit_solution(4254857301011018678)
XLA Ops:
  0.6 110.7 %paged_prefill.1 = (bf16[1024,512]{1,0:T(8,128)(2,1)}, bf16[1536,256]{1,0:T(8,128)(2,1)}) custom-call(bf16[128,4096]{1,0:T(8,128)(2,1)} %q_hbm.1, bf16[128,1024]{1,0:T(8,128)(2,1)} %k_hbm.1, bf16[128,1024]{1,0:T(8,128)(2,1)} %v_hbm.1, f32[1,128]{1,0:T(1,128)} %bitcast.6, f32[1,128]{1,0:T(1,128)} %bitcast.7, f32[1,128]{1,0:T(1,128)} %constant.2.clone.freq_ref, ...), custom_call_target="tpu_custom_call" | custom-call | tf_op jit(solution)/shard_map/paged_prefill/pallas_call | solution.py:448
  111.3 0.0 copy-start
  111.3 2.3 %copy.13 = bf16[1024,512]{1,0:T(8,128)(2,1)} copy(bf16[1024,512]{1,0:T(8,128)(2,1)} %get-tuple-element.10) | data formatting | bytes 2097152
  113.6 0.0 copy-done
  113.6 0.9 copy.14
Async XLA Ops:
  111.3 2.3 %copy-start = (bf16[1536,256]{1,0:T(8,128)(2,1)S(1)}, bf16[1536,256]{1,0:T(8,128)(2,1)}, u32[]{:S(2)}) copy-start(bf16[1536,256]{1,0:T(8,128)(2,1)} %get-tuple-element.5) | copy-start | bytes 2359300

commit v2 on v1

v2 whole, which is shorter than its diff:
```python
import functools
import math

import jax
import jax.numpy as jnp
import numpy as np
from jax import lax
from jax.experimental import pallas as pl
from jax.experimental.pallas import tpu as pltpu
from jax.sharding import PartitionSpec as P

D = 128
REACH = 4
PAGE = 16
GROUP = 4
PEERS = 8
FAR = -1e30
MESH = pl.DeviceIdType.MESH
NT = (((1,), (1,)), ((), ()))
FAR_SENDS = (4, 5, 6, 7)


def kernel(
    n_tok,
    q_hbm,
    k_hbm,
    v_hbm,
    qg_ref,
    kg_ref,
    freq_ref,
    len_ref,
    slot_ref,
    out_hbm,
    pool_hbm,
    qin,
    kin,
    vin,
    kvs,
    qs,
    kv,
    qbuf,
    kv_relay,
    q_relay,
    augk,
    augq,
    acc,
    total_ref,
    peak,
    ostage,
    pstage,
    in_sem,
    own_sem,
    out_sem,
    kv_send,
    kv_recv,
    q_send,
    q_recv,
    kv_on,
    kv_mid,
    q_on,
    q_mid,
    z_send,
    z_recv,
    s_send,
    s_recv,
):
    rows = kin.shape[0]
    shard = rows * PEERS
    half = shard // 2
    segs = len_ref.shape[0]
    tok = lax.axis_index("tok")
    head = lax.axis_index("head")
    hi, x = head // 4, lax.rem(head, 4)
    core = lax.rem(tok, 2)
    sibling = tok + 1 - 2 * core
    base = tok * shard

    run = n_tok // 4
    y = hi * 4 + tok // run
    at_run = lax.rem(tok, run)
    ending = at_run >= run - 2
    ahead = (at_run >= run - 4) & (at_run < run - 2) & (tok + 4 < n_tok)
    opened = (at_run < 2) & (tok >= 4)

    def device(col, row):
        row = lax.rem(row + 8, 8)
        return (lax.rem(row, 4) * run + at_run, row // 4 * 4 + lax.rem(col + 8, 4))

    def dest(n):
        return (hi if n < 4 else 1 - hi) * 4 + lax.rem(x - n + 8, 4)

    def origin(n):
        return lax.rem(hi + n // 4, 2) * 4 + lax.rem(x + n, 4)

    def way(n):
        return 2 if n % 2 == 0 else -2

    crossing = at_run >= run - 4

    def query_way(n):
        return jnp.where(crossing, -2, 2) if n == 6 else way(n)

    def rows_of(chunk):
        return pl.ds(pl.multiple_of(chunk * rows, rows), rows)

    barrier = pltpu.get_barrier_semaphore()

    def greet(where):
        pl.semaphore_signal(barrier, device_id=where, device_id_type=MESH)

    for n in (1, 2, 3):
        greet((tok, dest(n)))
    for n in FAR_SENDS:
        greet(device(x - n, y + way(n)))
        greet(device(x + n, y - way(n)))
    greet(device(x - 6, y - way(6)))
    greet(device(x + 6, y + way(6)))
    greet(device(x, y + 2))
    greet(device(x, y - 2))
    greet((sibling, head))

    @pl.when(tok + 2 < n_tok)
    def _():
        greet((tok + 2, head))

    @pl.when(tok >= 2)
    def _():
        greet((tok - 2, head))

    @pl.when(ahead)
    def _():
        greet((tok + 4, head))

    @pl.when(opened)
    def _():
        greet((tok - 4, head))

    loads = [
        pltpu.make_async_copy(k_hbm, kin, in_sem.at[0]),
        pltpu.make_async_copy(v_hbm, vin, in_sem.at[1]),
        pltpu.make_async_copy(q_hbm, qin, in_sem.at[2]),
    ]
    for load in loads:
        load.start()

    lane = lax.broadcasted_iota(jnp.int32, (1, D), 1)
    starts = jnp.full((1, D), 1 << 30, jnp.int32)
    ends = starts
    total = jnp.int32(0)
    for s in range(segs):
        starts = jnp.where(lane == s, total, starts)
        total = total + len_ref[s]
        ends = jnp.where(lane == s, total, ends)

    place = base + head * rows + lax.broadcasted_iota(jnp.int32, (rows, 1), 0)
    inside = (place >= starts) & (place < ends)
    first = jnp.sum(jnp.where(inside, starts.astype(jnp.float32), 0.0), axis=1, keepdims=True)
    angle = (place.astype(jnp.float32) - first) * freq_ref[...]
    cosine = jnp.cos(angle)
    sine = jnp.sin(angle)
    sine = jnp.where(lax.broadcasted_iota(jnp.int32, (rows, D), 1) < D // 2, -sine, sine)

    def rotated(tensor, gain):
        tensor = tensor.astype(jnp.float32)
        power = jnp.mean(tensor * tensor, axis=1, keepdims=True)
        tensor = tensor * lax.rsqrt(power + 1e-6) * gain
        return (tensor * cosine + pltpu.roll(tensor, D // 2, 1) * sine).astype(jnp.bfloat16)

    loads[0].wait()
    for g in range(PEERS):
        kvs[g, 0] = rotated(kin[:, g * D : (g + 1) * D], kg_ref[...])
    loads[1].wait()
    for g in range(PEERS):
        kvs[g, 1] = vin[:, g * D : (g + 1) * D]

    guests = (tok >= 2, tok + 2 < n_tok, ahead, opened)
    pl.semaphore_wait(barrier, 16 + sum(g.astype(jnp.int32) for g in guests))

    def own_rows(head_index):
        return pl.ds(pl.multiple_of(REACH * shard + head_index * rows, rows), rows)

    def remote(source, target, send, recv, where):
        return pltpu.make_async_remote_copy(
            src_ref=source,
            dst_ref=target,
            send_sem=send,
            recv_sem=recv,
            device_id=where,
            device_id_type=MESH,
        )

    kv_copies = [pltpu.make_async_copy(kvs.at[head], kv.at[:, own_rows(head)], own_sem.at[0])]
    q_copies = [pltpu.make_async_copy(qs.at[head], qbuf.at[0], own_sem.at[1])]
    for n in (1, 2, 3):
        where = (tok, dest(n))
        kv_copies.append(
            remote(kvs.at[dest(n)], kv.at[:, own_rows(head)], kv_send.at[n], kv_recv.at[n], where)
        )
        q_copies.append(remote(qs.at[dest(n)], qbuf.at[n], q_send.at[n], q_recv.at[n], where))
    kv_passes, q_passes = {}, {}
    for n in FAR_SENDS:
        k = n - 4
        where = device(x - n, y + way(n))
        kv_copies.append(remote(kvs.at[dest(n)], kv_relay.at[k], kv_send.at[n], kv_mid.at[k], where))
        there = device(x - n, y + query_way(n))
        q_copies.append(remote(qs.at[dest(n)], q_relay.at[k], q_send.at[n], q_mid.at[k], there))
        where = device(x, y + way(n))
        origin_head = device(x + n, y - way(n))[1]
        kv_passes[n] = remote(
            kv_relay.at[k], kv.at[:, own_rows(origin_head)], kv_on.at[k], kv_recv.at[n], where
        )
        there = device(x, y + query_way(n))
        q_passes[n] = remote(q_relay.at[k], qbuf.at[n], q_on.at[k], q_recv.at[n], there)
    for n in (4, 5, 6, 7, 1, 2, 3, 0):
        kv_copies[n].start()

    loads[2].wait()

    def turn_queries(n, carry):
        g = lax.rem(hi + n // 4, 2) * 4 + lax.rem(x - n + 8, 4)
        for r in range(GROUP):
            cols = pl.ds(pl.multiple_of((g * GROUP + r) * D, D), D)
            qs[g, r * rows : (r + 1) * rows] = rotated(qin[:, cols], qg_ref[...])
        return carry

    def slot_rows(d, part):
        return pl.ds(pl.multiple_of((REACH - d) * shard + part * half, half), half)

    parts = (hi, 1 - hi)

    def along(src_slot, dst_slot, which, index):
        return remote(
            kv.at[:, slot_rows(src_slot, parts[which])],
            kv.at[:, slot_rows(dst_slot, parts[which])],
            z_send.at[index],
            z_recv.at[dst_slot - 2 + which],
            (tok + (dst_slot - src_slot), head),
        )

    def across(src_slot, dst_slot, which):
        index = dst_slot - 1 + which
        return remote(
            kv.at[:, slot_rows(src_slot, parts[which])],
            kv.at[:, slot_rows(dst_slot, parts[which])],
            s_send.at[index],
            s_recv.at[index],
            (sibling, head),
        )

    def along_own(which):
        return along(0, 2, which, which)

    def along_on(which):
        return along(2, 4, which, 2 + which)

    def along_far(which):
        return along(0, 4, which, 4 + which)

    has_next = tok + 2 < n_tok
    passes = has_next & (tok >= 2) & jnp.logical_not(ending)

    def give_own(which):
        @pl.when(has_next)
        def _():
            along_own(which).start()

        @pl.when(ahead)
        def _():
            along_far(which).start()

        @pl.when(core == 0)
        def _():
            across(0, 1, which).start()

    def give_on(which):
        @pl.when(passes)
        def _():
            along_on(which).start()

        @pl.when((core == 1) & (tok >= 2))
        def _():
            across(2, 1, which).start()

        @pl.when((core == 0) & (tok >= 2))
        def _():
            across(2, 3, which).start()

    for d in range(1, REACH + 1):

        @pl.when(tok < d)
        def _(d=d):
            kv[:, (REACH - d) * shard : (REACH - d + 1) * shard] = jnp.zeros((2, shard, D), jnp.bfloat16)

    straight = jnp.logical_not(crossing)
    late = at_run < 2

    def pass_queries(n):
        q_copies[n].wait_recv()
        q_passes[n].start()

    def halo_on(which):
        @pl.when(tok >= 2)
        def _():
            along_own(which).wait_recv()

        give_on(which)

    lax.fori_loop(4, 6, turn_queries, 0)

    @pl.when(straight)
    def _():
        q_copies[4].start()
        q_copies[5].start()

    for n in (1, 2, 3):
        kv_copies[n].wait_recv()
    kv_copies[0].wait()
    give_own(0)
    for n in FAR_SENDS:
        kv_copies[n].wait_recv()
        kv_passes[n].start()
    lax.fori_loop(6, 8, turn_queries, 0)

    @pl.when(straight)
    def _():
        q_copies[6].start()
        q_copies[7].start()

    lax.fori_loop(0, 4, turn_queries, 0)
    for n in (1, 2, 3, 0):
        q_copies[n].start()

    @pl.when(jnp.logical_not(late))
    def _():
        halo_on(0)

    def mark_keys(index, carry):
        point = base - REACH * shard + index * rows + lax.broadcasted_iota(jnp.int32, (rows, 1), 0)
        within = (point >= starts) & (point < ends)
        augk[rows_of(index)] = jnp.where(within, 0.0, FAR).astype(jnp.bfloat16)
        return carry

    lax.fori_loop(0, (REACH + 1) * PEERS, mark_keys, 0)

    def mark_queries(index, carry):
        point = base + index * rows + lax.broadcasted_iota(jnp.int32, (rows, 1), 0)
        within = (point >= starts) & (point < ends)
        augq[rows_of(index)] = jnp.where(within, 1.0, 0.0).astype(jnp.bfloat16)
        return carry

    lax.fori_loop(0, PEERS, mark_queries, 0)

    for n in FAR_SENDS:
        kv_passes[n].wait_recv()
    give_own(1)

    @pl.when(crossing)
    def _():
        for n in FAR_SENDS:
            q_copies[n].start()
        halo_on(1)

    for n in FAR_SENDS:
        pass_queries(n)

    @pl.when(late)
    def _():
        halo_on(0)

    @pl.when(straight)
    def _():
        halo_on(1)

    scale = math.log2(math.e) / math.sqrt(D)

    def attend(n, begins, opening, closing):
        chunk = origin(n)
        mark = augq[rows_of(chunk)]
        query = jnp.concatenate([qbuf[n], jnp.concatenate([mark] * GROUP, axis=0)], axis=1)
        runs = [(begin, shard) for begin in begins]
        if opening:
            runs = [(REACH * shard, rows)] + runs

        def keys_at(index):
            begin, length = runs[index]
            return pl.ds(pl.multiple_of(chunk * rows + begin, rows), length)

        def front(index):
            at = keys_at(index)
            key = jnp.concatenate([kv[0, at], augk[at]], axis=1)
            score = lax.dot_general(query, key, NT, preferred_element_type=jnp.float32)
            if opening and index == 0:
                query_row = lax.rem(lax.broadcasted_iota(jnp.int32, score.shape, 0), rows)
                key_row = lax.broadcasted_iota(jnp.int32, score.shape, 1)
                score = jnp.where(key_row <= query_row, score, FAR)
            return score, jnp.broadcast_to(jnp.max(score, axis=1, keepdims=True), (GROUP * rows, D))

        ready = front(0)
        old = None if opening else peak[n]
        for index, (_, length) in enumerate(runs):
            score, top = ready
            if index + 1 < len(runs):
                ready = front(index + 1)
            if old is not None:
                top = jnp.maximum(old, top)
            expo = jnp.exp2((score - jnp.concatenate([top] * (length // D), axis=1)) * scale)
            part = expo[:, :D]
            for piece in range(1, length // D):
                part = part + expo[:, piece * D : (piece + 1) * D]
            mixed = jnp.dot(
                expo.astype(jnp.bfloat16), kv[1, keys_at(index)], preferred_element_type=jnp.float32
            )
            if old is None:
                acc[n] = mixed
                total_ref[n] = part
            else:
                factor = jnp.exp2((old - top) * scale)
                acc[n] = acc[n] * factor + mixed
                total_ref[n] = total_ref[n] * factor + part
            old = top
        if closing:
            done = acc[n] / jnp.sum(total_ref[n], axis=1, keepdims=True)
            done = done.astype(jnp.bfloat16)
            for r in range(GROUP):
                ostage[n, :, r * D : (r + 1) * D] = done[r * rows : (r + 1) * rows]
            out_copy(n).start()
        else:
            peak[n] = old

    def out_copy(n):
        return pltpu.make_async_copy(ostage.at[n], out_hbm.at[rows_of(origin(n))], out_sem.at[n])

    q_copies[0].wait()
    for n in (1, 2, 3):
        q_copies[n].wait_recv()

    for which in (0, 1):

        @pl.when(tok >= 1)
        def _(which=which):
            across(0, 1, which).wait_recv()

    def near_first(n, carry):
        attend(n, (3 * shard, 2 * shard), True, False)

        return carry

    lax.fori_loop(0, 4, near_first, 0)

    width = shard + 128
    spot = lax.broadcasted_iota(jnp.int32, (1, width), 1)
    point = base + spot - jnp.where(spot < shard, 0, width)
    begun = jnp.zeros((1, width), jnp.int32)
    ended = begun
    paged = begun
    total = jnp.int32(0)
    pages = jnp.int32(0)
    origin_rank = jnp.int32(0)
    for s in range(segs):
        length = len_ref[s]
        after = point >= total
        begun = jnp.where(after, total, begun)
        ended = jnp.where(after, total + length, ended)
        paged = jnp.where(after, pages, paged)
        origin_rank = jnp.where(base >= total, pages + lax.shift_right_logical(jnp.maximum(base - total, 0), 4), origin_rank)
        total = total + length
        pages = pages + lax.shift_right_logical(length + (PAGE - 1), 4)
    offset = jnp.maximum(point - begun, 0)
    block = lax.shift_right_logical(offset, 4)
    last = jnp.minimum(begun + (block + 1) * PAGE, ended) - 1
    owned = (point >= 0) & (last >= base) & (last < base + shard)
    wanted = jnp.where(owned, (paged + block - origin_rank) * PAGE + (offset & (PAGE - 1)), -1)

    pool_rows = pstage.shape[0]
    piece = 256
    slots = slot_ref[...]
    ranks = lax.broadcasted_iota(jnp.int32, slots.shape, 1).astype(jnp.float32)

    def fill(index, carry):
        row = index * piece + lax.broadcasted_iota(jnp.int32, (piece, 1), 0)
        rank = jnp.sum(jnp.where(slots == lax.shift_right_logical(row, 4), ranks, 0.0), axis=1, keepdims=True)
        code = rank.astype(jnp.int32) * PAGE + (row & (PAGE - 1))
        pick = jnp.where(code == wanted, 1.0, 0.0).astype(jnp.bfloat16)
        own = pl.ds(REACH * shard, shard)
        tail = pl.ds(REACH * shard - 128, 128)
        to = pl.ds(pl.multiple_of(index * piece, piece), piece)
        for plane in (0, 1):
            rowset = jnp.concatenate([kv[plane, own], kv[plane, tail]], axis=0)
            got = jnp.dot(pick, rowset, preferred_element_type=jnp.float32)
            pstage[to, plane * D : (plane + 1) * D] = got.astype(jnp.bfloat16)
        return carry

    lax.fori_loop(0, pool_rows // piece, fill, 0)
    pool_copy = pltpu.make_async_copy(pstage, pool_hbm, own_sem.at[2])
    pool_copy.start()

    for which in (0, 1):

        @pl.when(tok >= 4)
        def _(which=which):
            along_on(which).wait_recv()

        @pl.when((core == 1) & (tok >= 4))
        def _(which=which):
            across(4, 3, which).start()

    for which in (0, 1):

        @pl.when(tok >= 3)
        def _(which=which):
            across(2, 3, which).wait_recv()

    def near_last(n, carry):
        attend(n, (shard, 0), False, True)
        return carry

    lax.fori_loop(0, 4, near_last, 0)

    def far(n, carry):
        remote(q_relay.at[0], qbuf.at[n], q_on.at[0], q_recv.at[n], (sibling, head)).wait_recv()
        attend(n, (3 * shard, 2 * shard, shard, 0), True, True)
        return carry

    lax.fori_loop(4, PEERS, far, 0)

    for n in range(1, PEERS):
        kv_copies[n].wait_send()
        q_copies[n].wait_send()
    for n in FAR_SENDS:
        kv_passes[n].wait_send()
        q_passes[n].wait_send()
    for which in (0, 1):

        @pl.when(has_next)
        def _(which=which):
            along_own(which).wait_send()

        @pl.when(passes)
        def _(which=which):
            along_on(which).wait_send()

        @pl.when(ahead)
        def _(which=which):
            along_far(which).wait_send()

        @pl.when((core == 0) | (tok >= 2))
        def _(which=which):
            across(0, 1, which).wait_send()

        @pl.when(((core == 0) & (tok >= 2)) | ((core == 1) & (tok >= 4)))
        def _(which=which):
            across(2, 3, which).wait_send()

    for n in range(PEERS):
        out_copy(n).wait()
    pool_copy.wait()


def on_device(queries, key_states, value_states, query_gain, key_gain, lengths, slot_order):
    rows = queries.shape[0]
    shard = rows * PEERS
    slots = slot_order.shape[1]
    frequency = np.exp(np.arange(D // 2) * (-2.0 * math.log(1000000.0) / D)).astype(np.float32)
    frequency = jnp.asarray(np.concatenate([frequency, frequency])[None, :])
    vmem = pl.BlockSpec(memory_space=pltpu.VMEM)
    smem = pl.BlockSpec(memory_space=pltpu.SMEM)
    anywhere = pl.BlockSpec(memory_space=pl.ANY)
    bf16 = jnp.bfloat16
    dma = pltpu.SemaphoreType.DMA
    attention, pool = pl.pallas_call(
        functools.partial(kernel, lax.axis_size("tok")),
        out_shape=(
            jax.ShapeDtypeStruct((shard, GROUP * D), bf16),
            jax.ShapeDtypeStruct((slots * PAGE, 2 * D), bf16),
        ),
        in_specs=[anywhere, anywhere, anywhere, vmem, vmem, vmem, smem, vmem],
        out_specs=(anywhere, anywhere),
        scratch_shapes=[
            pltpu.VMEM((rows, PEERS * GROUP * D), bf16),
            pltpu.VMEM((rows, PEERS * D), bf16),
            pltpu.VMEM((rows, PEERS * D), bf16),
            pltpu.VMEM((PEERS, 2, rows, D), bf16),
            pltpu.VMEM((PEERS, GROUP * rows, D), bf16),
            pltpu.VMEM((2, (REACH + 1) * shard, D), bf16),
            pltpu.VMEM((PEERS, GROUP * rows, D), bf16),
            pltpu.VMEM((4, 2, rows, D), bf16),
            pltpu.VMEM((4, GROUP * rows, D), bf16),
            pltpu.VMEM(((REACH + 1) * shard, D), bf16),
            pltpu.VMEM((shard, D), bf16),
            pltpu.VMEM((PEERS, GROUP * rows, D), jnp.float32),
            pltpu.VMEM((PEERS, GROUP * rows, D), jnp.float32),
            pltpu.VMEM((PEERS, GROUP * rows, D), jnp.float32),
            pltpu.VMEM((PEERS, rows, GROUP * D), bf16),
            pltpu.VMEM((slots * PAGE, 2 * D), bf16),
            dma((3,)),
            dma((3,)),
            dma((PEERS,)),
            dma((PEERS,)),
            dma((PEERS,)),
            dma((PEERS,)),
            dma((PEERS,)),
            dma((4,)),
            dma((4,)),
            dma((4,)),
            dma((4,)),
            dma((6,)),
            dma((4,)),
            dma((4,)),
            dma((4,)),
        ],
        compiler_params=pltpu.CompilerParams(
            collective_id=0, has_side_effects=True, vmem_limit_bytes=56 * 2**20
        ),
        name="paged_prefill",
    )(
        queries,
        key_states,
        value_states,
        query_gain[None, :],
        key_gain[None, :],
        frequency,
        lengths,
        slot_order,
    )
    return attention, pool.reshape(slots, PAGE, 1, 2 * D)


def solution(mesh):
    in_specs = (
        P(("tok", "head"), None),
        P(("tok", "head"), None),
        P(("tok", "head"), None),
        P(),
        P(),
        P(),
        P("tok", None),
    )
    out_specs = (P("tok", "head"), P("tok", None, "head", None))
    return jax.shard_map(
        on_device, mesh=mesh, in_specs=in_specs, out_specs=out_specs, check_vma=False
    )
```

time: 115 us -> 90.3 us (0.79)
  the two profiles are of different devices: /device:TPU:52 before, /device:TPU:426 now
where the time goes in v2:
time: 90.3 us; the launch traced here: 90.1 us
  Pallas kernels  86.2 us (95%)
  local copies, waits for them, and re-layouts  3.22 us (4%)
    pallas_call x1, Pallas kernels, on_device(): pl.pallas_call(functools.partial(kernel, lax.axis_size('tok')), out_shape...  86.2 us
    unnamed x4, local copies, waits for them, and re-layouts  3.22 us

profile of v2, /device:TPU:426, one launch (start us, length us, event | category | flops | bytes accessed | tf_op | source)
XLA Modules:
  0.0 90.1 jit_solution(6354877104172910353)
XLA Ops:
  0.6 86.2 %paged_prefill.1 = (bf16[1024,512]{1,0:T(8,128)(2,1)}, bf16[1536,256]{1,0:T(8,128)(2,1)}) custom-call(bf16[128,4096]{1,0:T(8,128)(2,1)} %q_hbm.1, bf16[128,1024]{1,0:T(8,128)(2,1)} %k_hbm.1, bf16[128,1024]{1,0:T(8,128)(2,1)} %v_hbm.1, f32[1,128]{1,0:T(1,128)} %bitcast.6, f32[1,128]{1,0:T(1,128)} %bitcast.7, f32[1,128]{1,0:T(1,128)} %constant.2.clone.freq_ref, ...), custom_call_target="tpu_custom_call" | custom-call | tf_op jit(solution)/shard_map/paged_prefill/pallas_call | solution.py:570
  86.9 0.0 copy-start
  86.9 2.3 %copy.13 = bf16[1024,512]{1,0:T(8,128)(2,1)} copy(bf16[1024,512]{1,0:T(8,128)(2,1)} %get-tuple-element.10) | data formatting | bytes 2097152
  89.2 0.0 copy-done
  89.2 0.9 copy.14
Async XLA Ops:
  86.9 2.3 %copy-start = (bf16[1536,256]{1,0:T(8,128)(2,1)S(1)}, bf16[1536,256]{1,0:T(8,128)(2,1)}, u32[]{:S(2)}) copy-start(bf16[1536,256]{1,0:T(8,128)(2,1)} %get-tuple-element.5) | copy-start | bytes 2359300

commit v3 on v2

--- a/solution.py
+++ b/solution.py
@@ -41,6 +41,7 @@
     qbuf,
     kv_relay,
     q_relay,
+    halo_relay,
     augk,
     augq,
     acc,
@@ -61,6 +62,8 @@
     q_mid,
     z_send,
     z_recv,
+    turn_send,
+    turn_recv,
     s_send,
     s_recv,
 ):
@@ -81,6 +84,7 @@
     ending = at_run >= run - 2
     ahead = (at_run >= run - 4) & (at_run < run - 2) & (tok + 4 < n_tok)
     opened = (at_run < 2) & (tok >= 4)
+    between = (at_run // 2 == 3) & (tok + 10 < n_tok)
 
     def device(col, row):
         row = lax.rem(row + 8, 8)
@@ -95,7 +99,7 @@
     def way(n):
         return 2 if n % 2 == 0 else -2
 
-    crossing = at_run >= run - 4
+    crossing = at_run >= run - 2
 
     def query_way(n):
         return jnp.where(crossing, -2, 2) if n == 6 else way(n)
@@ -129,11 +133,16 @@
 
     @pl.when(ahead)
     def _():
-        greet((tok + 4, head))
+        greet((tok - 6, head))
+
+    @pl.when(between)
+    def _():
+        greet((tok + 6, head))
+        greet((tok + 10, head))
 
     @pl.when(opened)
     def _():
-        greet((tok - 4, head))
+        greet((tok - 10, head))
 
     loads = [
         pltpu.make_async_copy(k_hbm, kin, in_sem.at[0]),
@@ -173,7 +182,7 @@
     for g in range(PEERS):
         kvs[g, 1] = vin[:, g * D : (g + 1) * D]
 
-    guests = (tok >= 2, tok + 2 < n_tok, ahead, opened)
+    guests = (tok >= 2, tok + 2 < n_tok, ahead, opened, between, between)
     pl.semaphore_wait(barrier, 16 + sum(g.astype(jnp.int32) for g in guests))
 
     def own_rows(head_index):
@@ -253,8 +262,29 @@
     def along_on(which):
         return along(2, 4, which, 2 + which)
 
-    def along_far(which):
-        return along(0, 4, which, 4 + which)
+    def far_out(which):
+        return remote(
+            kv.at[:, slot_rows(0, parts[which])],
+            halo_relay.at[which],
+            z_send.at[4 + which],
+            turn_recv.at[which],
+            (tok - 6, head),
+        )
+
+    def far_on(which):
+        return remote(
+            halo_relay.at[which],
+            kv.at[:, slot_rows(4, parts[which])],
+            turn_send.at[which],
+            z_recv.at[2 + which],
+            (tok + 10, head),
+        )
+
+    def turn(which):
+        @pl.when(between)
+        def _():
+            far_out(which).wait_recv()
+            far_on(which).start()
 
     has_next = tok + 2 < n_tok
     passes = has_next & (tok >= 2) & jnp.logical_not(ending)
@@ -266,7 +296,7 @@
 
         @pl.when(ahead)
         def _():
-            along_far(which).start()
+            far_out(which).start()
 
         @pl.when(core == 0)
         def _():
@@ -334,6 +364,8 @@
     def _():
         halo_on(0)
 
+    turn(0)
+
     def mark_keys(index, carry):
         point = base - REACH * shard + index * rows + lax.broadcasted_iota(jnp.int32, (rows, 1), 0)
         within = (point >= starts) & (point < ends)
@@ -370,6 +402,8 @@
     @pl.when(straight)
     def _():
         halo_on(1)
+
+    turn(1)
 
     scale = math.log2(math.e) / math.sqrt(D)
 
@@ -541,7 +575,11 @@
 
         @pl.when(ahead)
         def _(which=which):
-            along_far(which).wait_send()
+            far_out(which).wait_send()
+
+        @pl.when(between)
+        def _(which=which):
+            far_on(which).wait_send()
 
         @pl.when((core == 0) | (tok >= 2))
         def _(which=which):
@@ -585,6 +623,7 @@
             pltpu.VMEM((PEERS, GROUP * rows, D), bf16),
             pltpu.VMEM((4, 2, rows, D), bf16),
             pltpu.VMEM((4, GROUP * rows, D), bf16),
+            pltpu.VMEM((2, 2, shard // 2, D), bf16),
             pltpu.VMEM(((REACH + 1) * shard, D), bf16),
             pltpu.VMEM((shard, D), bf16),
             pltpu.VMEM((PEERS, GROUP * rows, D), jnp.float32),
@@ -605,6 +644,8 @@
             dma((4,)),
             dma((6,)),
             dma((4,)),
+            dma((2,)),
+            dma((2,)),
             dma((4,)),
             dma((4,)),
         ],

time: 90.3 us -> 86.1 us (0.953)
  the two profiles are of different devices: /device:TPU:426 before, /device:TPU:54 now
where the time goes in v3:
time: 86.1 us; the launch traced here: 85.9 us
  Pallas kernels  82 us (95%)
  local copies, waits for them, and re-layouts  3.22 us (4%)
    pallas_call x1, Pallas kernels, on_device(): pl.pallas_call(functools.partial(kernel, lax.axis_size('tok')), out_shape...  82 us
    unnamed x4, local copies, waits for them, and re-layouts  3.22 us

profile of v3, /device:TPU:54, one launch (start us, length us, event | category | flops | bytes accessed | tf_op | source)
XLA Modules:
  0.0 85.9 jit_solution(11411236470778768812)
XLA Ops:
  0.6 82.0 %paged_prefill.1 = (bf16[1024,512]{1,0:T(8,128)(2,1)}, bf16[1536,256]{1,0:T(8,128)(2,1)}) custom-call(bf16[128,4096]{1,0:T(8,128)(2,1)} %q_hbm.1, bf16[128,1024]{1,0:T(8,128)(2,1)} %k_hbm.1, bf16[128,1024]{1,0:T(8,128)(2,1)} %v_hbm.1, f32[1,128]{1,0:T(1,128)} %bitcast.6, f32[1,128]{1,0:T(1,128)} %bitcast.7, f32[1,128]{1,0:T(1,128)} %constant.2.clone.freq_ref, ...), custom_call_target="tpu_custom_call" | custom-call | tf_op jit(solution)/shard_map/paged_prefill/pallas_call | solution.py:608
  82.7 0.0 copy-start
  82.7 2.3 %copy.13 = bf16[1024,512]{1,0:T(8,128)(2,1)} copy(bf16[1024,512]{1,0:T(8,128)(2,1)} %get-tuple-element.10) | data formatting | bytes 2097152
  85.0 0.0 copy-done
  85.0 0.9 %copy.14 = bf16[96,16,1,256]{3,1,2,0:T(8,128)(2,1)} copy(bf16[96,16,1,256]{3,1,2,0:T(8,128)(2,1)S(1)} %bitcast.5) | data formatting | bytes 1572864
Async XLA Ops:
  82.7 2.3 %copy-start = (bf16[1536,256]{1,0:T(8,128)(2,1)S(1)}, bf16[1536,256]{1,0:T(8,128)(2,1)}, u32[]{:S(2)}) copy-start(bf16[1536,256]{1,0:T(8,128)(2,1)} %get-tuple-element.5) | copy-start | bytes 2359300

commit v4 on v3

--- a/solution.py
+++ b/solution.py
@@ -395,6 +395,60 @@
     for n in FAR_SENDS:
         pass_queries(n)
 
+    width = shard + 128
+    spot = lax.broadcasted_iota(jnp.int32, (1, width), 1)
+    point = base + spot - jnp.where(spot < shard, 0, width)
+    begun = jnp.zeros((1, width), jnp.int32)
+    ended = begun
+    paged = begun
+    total = jnp.int32(0)
+    pages = jnp.int32(0)
+    origin_rank = jnp.int32(0)
+    for s in range(segs):
+        length = len_ref[s]
+        after = point >= total
+        begun = jnp.where(after, total, begun)
+        ended = jnp.where(after, total + length, ended)
+        paged = jnp.where(after, pages, paged)
+        origin_rank = jnp.where(base >= total, pages + lax.shift_right_logical(jnp.maximum(base - total, 0), 4), origin_rank)
+        total = total + length
+        pages = pages + lax.shift_right_logical(length + (PAGE - 1), 4)
+    offset = jnp.maximum(point - begun, 0)
+    block = lax.shift_right_logical(offset, 4)
+    last = jnp.minimum(begun + (block + 1) * PAGE, ended) - 1
+    owned = (point >= 0) & (last >= base) & (last < base + shard)
+    wanted = jnp.where(owned, (paged + block - origin_rank) * PAGE + (offset & (PAGE - 1)), -1)
+
+    pool_rows = pstage.shape[0]
+    piece = 256
+    slots = slot_ref[...]
+    ranks = lax.broadcasted_iota(jnp.int32, slots.shape, 1).astype(jnp.float32)
+
+    def picked(index, low, high):
+        row = index * piece + lax.broadcasted_iota(jnp.int32, (piece, 1), 0)
+        rank = jnp.sum(jnp.where(slots == lax.shift_right_logical(row, 4), ranks, 0.0), axis=1, keepdims=True)
+        code = rank.astype(jnp.int32) * PAGE + (row & (PAGE - 1))
+        return jnp.where(code == wanted[:, low:high], 1.0, 0.0).astype(jnp.bfloat16)
+
+    def fill(index, carry):
+        pick = picked(index, 0, shard)
+        to = pl.ds(pl.multiple_of(index * piece, piece), piece)
+        for plane in (0, 1):
+            got = jnp.dot(pick, kv[plane, pl.ds(REACH * shard, shard)], preferred_element_type=jnp.float32)
+            pstage[to, plane * D : (plane + 1) * D] = got.astype(jnp.bfloat16)
+        return carry
+
+    def fill_tail(index, carry):
+        pick = picked(index, shard, width)
+        to = pl.ds(pl.multiple_of(index * piece, piece), piece)
+        for plane in (0, 1):
+            cols = slice(plane * D, (plane + 1) * D)
+            got = jnp.dot(pick, kv[plane, pl.ds(REACH * shard - 128, 128)], preferred_element_type=jnp.float32)
+            pstage[to, cols] = pstage[to, cols] + got.astype(jnp.bfloat16)
+        return carry
+
+    lax.fori_loop(0, pool_rows // piece, fill, 0)
+
     @pl.when(late)
     def _():
         halo_on(0)
@@ -481,50 +535,7 @@
 
     lax.fori_loop(0, 4, near_first, 0)
 
-    width = shard + 128
-    spot = lax.broadcasted_iota(jnp.int32, (1, width), 1)
-    point = base + spot - jnp.where(spot < shard, 0, width)
-    begun = jnp.zeros((1, width), jnp.int32)
-    ended = begun
-    paged = begun
-    total = jnp.int32(0)
-    pages = jnp.int32(0)
-    origin_rank = jnp.int32(0)
-    for s in range(segs):
-        length = len_ref[s]
-        after = point >= total
-        begun = jnp.where(after, total, begun)
-        ended = jnp.where(after, total + length, ended)
-        paged = jnp.where(after, pages, paged)
-        origin_rank = jnp.where(base >= total, pages + lax.shift_right_logical(jnp.maximum(base - total, 0), 4), origin_rank)
-        total = total + length
-        pages = pages + lax.shift_right_logical(length + (PAGE - 1), 4)
-    offset = jnp.maximum(point - begun, 0)
-    block = lax.shift_right_logical(offset, 4)
-    last = jnp.minimum(begun + (block + 1) * PAGE, ended) - 1
-    owned = (point >= 0) & (last >= base) & (last < base + shard)
-    wanted = jnp.where(owned, (paged + block - origin_rank) * PAGE + (offset & (PAGE - 1)), -1)
-
-    pool_rows = pstage.shape[0]
-    piece = 256
-    slots = slot_ref[...]
-    ranks = lax.broadcasted_iota(jnp.int32, slots.shape, 1).astype(jnp.float32)
-
-    def fill(index, carry):
-        row = index * piece + lax.broadcasted_iota(jnp.int32, (piece, 1), 0)
-        rank = jnp.sum(jnp.where(slots == lax.shift_right_logical(row, 4), ranks, 0.0), axis=1, keepdims=True)
-        code = rank.astype(jnp.int32) * PAGE + (row & (PAGE - 1))
-        pick = jnp.where(code == wanted, 1.0, 0.0).astype(jnp.bfloat16)
-        own = pl.ds(REACH * shard, shard)
-        tail = pl.ds(REACH * shard - 128, 128)
-        to = pl.ds(pl.multiple_of(index * piece, piece), piece)
-        for plane in (0, 1):
-            rowset = jnp.concatenate([kv[plane, own], kv[plane, tail]], axis=0)
-            got = jnp.dot(pick, rowset, preferred_element_type=jnp.float32)
-            pstage[to, plane * D : (plane + 1) * D] = got.astype(jnp.bfloat16)
-        return carry
-
-    lax.fori_loop(0, pool_rows // piece, fill, 0)
+    lax.fori_loop(0, pool_rows // piece, fill_tail, 0)
     pool_copy = pltpu.make_async_copy(pstage, pool_hbm, own_sem.at[2])
     pool_copy.start()
 

time: 86.1 us -> 86.1 us (level)
  no operation moved by 1% of the time
where the time goes in v4:
time: 86.1 us; the launch traced here: 85.9 us
  Pallas kernels  82 us (95%)
  local copies, waits for them, and re-layouts  3.22 us (4%)
    pallas_call x1, Pallas kernels, on_device(): pl.pallas_call(functools.partial(kernel, lax.axis_size('tok')), out_shape...  82 us
    unnamed x4, local copies, waits for them, and re-layouts  3.22 us

profile of v4, /device:TPU:54, one launch (start us, length us, event | category | flops | bytes accessed | tf_op | source)
XLA Modules:
  0.0 85.9 jit_solution(3670475797854884502)
XLA Ops:
  0.6 82.0 %paged_prefill.1 = (bf16[1024,512]{1,0:T(8,128)(2,1)}, bf16[1536,256]{1,0:T(8,128)(2,1)}) custom-call(bf16[128,4096]{1,0:T(8,128)(2,1)} %q_hbm.1, bf16[128,1024]{1,0:T(8,128)(2,1)} %k_hbm.1, bf16[128,1024]{1,0:T(8,128)(2,1)} %v_hbm.1, f32[1,128]{1,0:T(1,128)} %bitcast.6, f32[1,128]{1,0:T(1,128)} %bitcast.7, f32[1,128]{1,0:T(1,128)} %constant.2.clone.freq_ref, ...), custom_call_target="tpu_custom_call" | custom-call | tf_op jit(solution)/shard_map/paged_prefill/pallas_call | solution.py:619
  82.7 0.0 copy-start
  82.7 2.3 %copy.13 = bf16[1024,512]{1,0:T(8,128)(2,1)} copy(bf16[1024,512]{1,0:T(8,128)(2,1)} %get-tuple-element.10) | data formatting | bytes 2097152
  85.0 0.0 copy-done
  85.0 0.9 %copy.14 = bf16[96,16,1,256]{3,1,2,0:T(8,128)(2,1)} copy(bf16[96,16,1,256]{3,1,2,0:T(8,128)(2,1)S(1)} %bitcast.5) | data formatting | bytes 1572864
Async XLA Ops:
  82.7 2.3 %copy-start = (bf16[1536,256]{1,0:T(8,128)(2,1)S(1)}, bf16[1536,256]{1,0:T(8,128)(2,1)}, u32[]{:S(2)}) copy-start(bf16[1536,256]{1,0:T(8,128)(2,1)} %get-tuple-element.5) | copy-start | bytes 2359300
